TPU v7x, 256 devices: a whole 4x4x8 slice. The times are simulated.
256 devices in a mesh: row: 32 (over x, z_lo, y), col: 8 (over z_hi, core).
Axes of the slice: x: 4, y: 4, z: 8 (z_hi: 4, z_lo: 2; z = z_hi * 2 + z_lo), core: 2. Of those that a mesh axis runs over, the one named last changes fastest.
Arguments:
- root_cov: float32 [6144, 6144], P('row', 'col'), as said below
- structure: int32 [16], replicated, may hold values from 0 to 47
- child_factor: float32 [2048, 4096], P('row', 'col'), may hold values from -0.9 to 0.9
- child_diag: float32 [4096, 4096], P('row', 'col'), may hold values from -6 to 6
Outputs:
- cross_cov: float32 [2048, 4096], P('row', 'col')
- child_cov: float32 [4096, 4096], P('row', 'col')
Inputs may be any that keep to these rules, and one draw needn't show every extreme that they name: root_cov is exactly symmetric and positive definite; its off-diagonal entries are small against its diagonal, which is about 1.5 times the product of a row scale and a column scale.
All inputs are finite; a program needn't handle non-finite values.
Results may differ from a plain program's by a relative error of at most 0.000078.
Values sent between devices are 32-bit elements; how exact they have to be, the bound alone decides.
No kernel may reach another device: no remote copies, remote signals or barrier semaphores. Data moves between devices by JAX's collectives and lax.ppermute only.
A program may use at most 64 MiB of HBM per device.

v0:
```python
import jax
import jax.numpy as jnp
from jax import lax
from jax.sharding import PartitionSpec as P

BLK = 128


def contract_rows(first_mat, second_mat):
    return lax.dot_general(
        first_mat,
        second_mat,
        (((0,), (0,)), ((), ())),
        precision=lax.Precision.HIGHEST,
        preferred_element_type=jnp.float32,
    )


def per_device(root_cov, structure, child_factor, child_diag):
    rows_dev = root_cov.shape[0]
    offsets = lax.iota(jnp.int32, BLK)
    struct_rows = (structure[:, None] * BLK + offsets[None, :]).reshape(-1)
    row_index = lax.axis_index("row")
    global_rows = row_index * rows_dev + lax.iota(jnp.int32, rows_dev)
    tile_index = global_rows // BLK
    rank_count = jnp.sum((structure[None, :] < tile_index[:, None]).astype(jnp.int32), axis=1)
    member = jnp.any(structure[None, :] == tile_index[:, None], axis=1)
    position = rank_count * BLK + global_rows % BLK
    shard_piece = lax.all_gather(root_cov, "col", axis=1, tiled=True)
    local_index = struct_rows
    inside = (local_index >= 0) & (local_index < shard_piece.shape[1])
    taken_rows = jnp.take(shard_piece, jnp.clip(local_index, 0, shard_piece.shape[1] - 1), axis=1)
    picked = jnp.where(inside[None, :], taken_rows, 0.0)
    shard_piece = lax.all_gather(child_factor, "row", axis=0, tiled=True)
    local_index = position
    inside = member & (local_index >= 0) & (local_index < shard_piece.shape[0])
    taken_rows = jnp.take(shard_piece, jnp.clip(local_index, 0, shard_piece.shape[0] - 1), axis=0)
    spread = jnp.where(inside[:, None], taken_rows, 0.0)
    cross_cov = lax.psum_scatter(
        -contract_rows(picked, spread), "row", scatter_dimension=0, tiled=True
    )
    factor_rows = lax.all_gather(child_factor, "col", axis=1, tiled=True)
    child_cov = child_diag + lax.psum_scatter(
        -contract_rows(factor_rows, cross_cov), "row", scatter_dimension=0, tiled=True
    )
    return (cross_cov, child_cov)


def solution(mesh):
    return jax.shard_map(
        per_device,
        mesh=mesh,
        in_specs=(P("row", "col"), P(), P("row", "col"), P("row", "col")),
        out_specs=(P("row", "col"), P("row", "col")),
        check_vma=False,
    )
```

profile of v0, /device:TPU:64, one launch (start us, length us, event | category | flops | bytes accessed | tf_op | source)
XLA Modules:
  0.0 641.2 jit_solution(759094218836384815)
XLA Ops:
  7.2 0.7 all-gather.6.cloned.1.call-update
  7.9 0.0 all-gather.4.cloned.1.call-start
  8.0 2.2 copy.12
  10.2 0.0 all-gather.8.cloned.1.call-start
  10.2 0.7 all-gather.8.cloned.1.call-update
  11.0 0.1 convert_reduce_fusion
  11.1 0.1 compare_reduce_fusion
  11.3 0.1 compare_and_fusion
  11.4 0.1 fusion.16
  11.4 0.1 fusion.12
  11.5 160.5 %all-gather.6.cloned.1.call-done = f32[2048,512]{1,0:T(8,128)} async-done(((f32[64,512]{1,0:T(8,128)}), f32[2048,512]{1,0:T(8,128)}) %all-gather.6.cloned.1.call-update) | async-done | bytes 4194320 | tf_op jit(solution)/shard_map/all_gather | solution.py:34
  172.1 3.2 gather_fusion.1
  175.3 67.9 %all-gather.4.cloned.1.call-done = f32[192,6144]{0,1:T(8,128)} async-done(((f32[192,768]{0,1:T(8,128)}), f32[192,6144]{0,1:T(8,128)}) %all-gather.4.cloned.1.call-update) | async-done | bytes 4718608 | tf_op jit(solution)/shard_map/all_gather | solution.py:29
  243.2 9.4 %gather_fusion = f32[2048,192]{1,0:T(8,128)S(1)} fusion(f32[192,6144]{0,1:T(8,128)} %all-gather.4.cloned.1.call-done, s32[2048]{0:T(1024)S(1)} %broadcast_clamp_fusion), kind=kCustom, calls=%fused_computation | custom fusion | bytes 3153920 | tf_op jit(solution)/shard_map/jit(_take)/gather | solution.py:32
  252.7 5.3 convolution_negate_fusion
  258.0 0.0 reduce-scatter.5.cloned.1.call-start
  258.0 14.9 %all-gather.8.cloned.1.call-done = f32[64,4096]{1,0:T(8,128)} async-done(((f32[64,512]{1,0:T(8,128)}), f32[64,4096]{1,0:T(8,128)}) %all-gather.8.cloned.1.call-update) | async-done | bytes 1048592 | tf_op jit(solution)/shard_map/all_gather | solution.py:42
  272.9 173.4 %reduce-scatter.3.cloned.1.call-done = f32[64,512]{1,0:T(8,128)} async-done(((f32[2048,512]{1,0:T(8,128)}), f32[64,512]{1,0:T(8,128)}) %reduce-scatter.3.cloned.1.call-update) | async-done | bytes 131088 | tf_op jit(solution)/shard_map/reduce_scatter | solution.py:39
  446.4 10.0 %negate_bitcast_fusion = f32[4096,512]{0,1:T(8,128)} fusion(f32[64,512]{1,0:T(8,128)} %reduce-scatter.3.cloned.1.call-done, f32[64,4096]{1,0:T(8,128)} %all-gather.8.cloned.1.call-done), kind=kOutput, calls=%fused_computation.2 | convolution fusion | flops 1612709888 | bytes 9568256 | tf_op jit(solution)/shard_map/dot_general | solution.py:10
  456.5 0.9 copy-done
  457.4 0.1 copy.13
  457.5 175.3 %reduce-scatter.5.cloned.1.call-done = f32[128,512]{0,1:T(8,128)} async-done(((f32[4096,512]{0,1:T(8,128)}), f32[128,512]{0,1:T(8,128)}) %reduce-scatter.5.cloned.1.call-update) | async-done | bytes 262160 | tf_op jit(solution)/shard_map/reduce_scatter | solution.py:43
  632.9 1.0 add.152
  633.8 0.8 copy.14
  (17 shorter events, 0.2 us)
Async XLA Ops:
  7.2 3.8 copy-start.1
  7.2 164.9 %all-gather.6.cloned.1.call-start = ((), (), s32[]{:S(2)}) async-start(), calls=%async_computation.3 | async-start | bytes 4325376 | tf_op jit(solution)/shard_map/all_gather | solution.py:34
  7.9 235.3 %all-gather.4.cloned.1.call-start = ((), (), s32[]{:S(2)}) async-start(), calls=%async_computation.2 | async-start | bytes 7077888 | tf_op jit(solution)/shard_map/all_gather | solution.py:29
  10.2 262.8 %all-gather.8.cloned.1.call-start = ((), (), s32[]{:S(2)}) async-start(), calls=%async_computation.5 | async-start | bytes 1179648 | tf_op jit(solution)/shard_map/all_gather | solution.py:42
  10.9 435.5 %reduce-scatter.3.cloned.1.call-start = ((), (), s32[]{:S(2)}) async-start(), calls=%async_computation.4 | async-start | bytes 4325376 | tf_op jit(solution)/shard_map/reduce_scatter | solution.py:39
  258.0 374.9 %reduce-scatter.5.cloned.1.call-start = ((), (), s32[]{:S(2)}) async-start(), calls=%async_computation.6 | async-start | bytes 8650752 | tf_op jit(solution)/shard_map/reduce_scatter | solution.py:43
  456.4 0.9 copy-start
Sparse Core Ops, SparseCore 0:
  9.8 162.2 all-gather.5
  173.9 69.2 all-gather.3
  245.1 27.8 all-gather.7
  275.9 170.4 reduce-scatter.2
  456.6 176.2 reduce-scatter.4
where the time goes:
time: 641 us
  waiting for transfers between devices  594 us (93%)
  local copies, waits for them, and re-layouts  16.8 us (3%)
  matrix products  15.3 us (2%)
  between operations  13.9 us (2%)
    reduce_scatter x1, waiting for transfers between devices, per_device(): lax.psum_scatter(-contract_rows(factor_rows, cross_cov), 'row', scatter_d...  175 us
    reduce_scatter x1, waiting for transfers between devices, per_device(): lax.psum_scatter(-contract_rows(picked, spread), 'row', scatter_dimension...  173 us
    all_gather x1, waiting for transfers between devices, per_device(): shard_piece = lax.all_gather(child_factor, 'row', axis=0, tiled=True)  161 us
    all_gather x1, waiting for transfers between devices, per_device(): shard_piece = lax.all_gather(root_cov, 'col', axis=1, tiled=True)  67.9 us
    dot_general x2, matrix products, contract_rows(): lax.dot_general(first_mat, second_mat, (((0,), (0,)), ((), ())), precisio...  15.3 us
    all_gather x1, waiting for transfers between devices, per_device(): factor_rows = lax.all_gather(child_factor, 'col', axis=1, tiled=True)  14.9 us
  transfers between devices with their start and end apart: 5, of which 5 were waited for; matrix products, arithmetic and copies ran while one was open for 3% of the time, Pallas kernels for 0%

commit v1 on v0

--- a/solution.py
+++ b/solution.py
@@ -4,6 +4,11 @@
 from jax.sharding import PartitionSpec as P
 
 BLK = 128
+
+
+def exchange_gather(value, mesh_axis, dim):
+    stack = jnp.stack([value] * lax.axis_size(mesh_axis))
+    return jnp.concatenate(lax.all_to_all(stack, mesh_axis, 0, 0), axis=dim)
 
 
 def contract_rows(first_mat, second_mat):
@@ -26,7 +31,7 @@
     rank_count = jnp.sum((structure[None, :] < tile_index[:, None]).astype(jnp.int32), axis=1)
     member = jnp.any(structure[None, :] == tile_index[:, None], axis=1)
     position = rank_count * BLK + global_rows % BLK
-    shard_piece = lax.all_gather(root_cov, "col", axis=1, tiled=True)
+    shard_piece = exchange_gather(root_cov, "col", 1)
     local_index = struct_rows
     inside = (local_index >= 0) & (local_index < shard_piece.shape[1])
     taken_rows = jnp.take(shard_piece, jnp.clip(local_index, 0, shard_piece.shape[1] - 1), axis=1)

time: 641 us -> 609 us (0.950)
  waiting for transfers between devices: 594 us -> 545 us
  starting transfers between devices: 0.2 us -> 8.37 us
  local copies, waits for them, and re-layouts: 16.8 us -> 24.4 us
    all_gather x1 -> x0, waiting for transfers between devices: 67.9 us -> none  [per_device(): shard_piece = lax.all_gather(root_cov, 'col', axis=1, tiled=True)]
    all_gather x1, waiting for transfers between devices: 161 us -> 189 us  [per_device(): shard_piece = lax.all_gather(child_factor, 'row', axis=0, tiled=True)]
    all_gather x1, waiting for transfers between devices: 14.9 us -> 5.43 us  [per_device(): factor_rows = lax.all_gather(child_factor, 'col', axis=1, tiled=True)]
    all_to_all x0 -> x1, starting transfers between devices: none -> 8.25 us  [exchange_gather(): return jnp.concatenate(lax.all_to_all(stack, mesh_axis, 0, 0), axis=dim)]
  transfers between devices with their start and end apart: 5 -> 5, of which waited for: 5 -> 4; matrix products, arithmetic and copies ran while one was open for 3% -> 5% of each run, Pallas kernels for 0% -> 0%
where the time goes in v1:
time: 609 us
  waiting for transfers between devices  545 us (89%)
  local copies, waits for them, and re-layouts  24.4 us (4%)
  matrix products  15.3 us (3%)
  between operations  13.9 us (2%)
  starting transfers between devices  8.37 us (1%)
    all_gather x1, waiting for transfers between devices, per_device(): shard_piece = lax.all_gather(child_factor, 'row', axis=0, tiled=True)  189 us
    reduce_scatter x1, waiting for transfers between devices, per_device(): lax.psum_scatter(-contract_rows(factor_rows, cross_cov), 'row', scatter_d...  176 us
    reduce_scatter x1, waiting for transfers between devices, per_device(): lax.psum_scatter(-contract_rows(picked, spread), 'row', scatter_dimension...  173 us
    dot_general x2, matrix products, contract_rows(): lax.dot_general(first_mat, second_mat, (((0,), (0,)), ((), ())), precisio...  15.3 us
  transfers between devices with their start and end apart: 5, of which 4 were waited for; matrix products, arithmetic and copies ran while one was open for 5% of the time, Pallas kernels for 0%

profile of v1, /device:TPU:64, one launch (start us, length us, event | category | flops | bytes accessed | tf_op | source)
XLA Modules:
  0.0 608.8 jit_solution(9139252617354833650)
XLA Ops:
  7.2 0.7 all-gather.3.cloned.1.call-update
  7.9 3.7 stack.2
  11.6 8.2 %all-to-all-start = ((f32[8,192,768]{2,1,0:T(8,128)}), f32[8,192,768]{2,1,0:T(8,128)}, u32[]{:S(2)}, u32[]{:S(2)}) async-start(f32[8,192,768]{2,1,0:T(8,128)} %stack.2), calls=%async_computation | async-start | bytes 9437184 | tf_op jit(solution)/shard_map/all_to_all | solution.py:11
  19.8 0.7 all-gather.5.cloned.1.call-update
  20.5 0.0 reduce-scatter.3.cloned.1.call-start
  20.6 0.1 convert_reduce_fusion
  20.7 0.1 compare_reduce_fusion
  20.9 0.1 fusion.16
  21.0 0.1 compare_and_fusion
  21.0 0.1 fusion.12
  21.1 189.1 %all-gather.3.cloned.1.call-done = f32[2048,512]{1,0:T(8,128)} async-done(((f32[64,512]{1,0:T(8,128)}), f32[2048,512]{1,0:T(8,128)}) %all-gather.3.cloned.1.call-update) | async-done | bytes 4194320 | tf_op jit(solution)/shard_map/all_gather | solution.py:39
  210.2 3.2 gather_fusion.1
  213.5 6.2 %copy.15 = f32[192,8,768]{0,2,1:T(8,128)} copy(f32[192,8,768]{2,0,1:T(8,128)} %bitcast.2) | data formatting | bytes 9437184 | tf_op jit(solution)/shard_map/reshape | solution.py:11
  219.7 9.5 %gather_fusion = f32[2048,192]{1,0:T(8,128)S(1)} fusion(f32[192,6144]{0,1:T(8,128)} %bitcast.16, s32[2048]{0:T(1024)S(1)} %broadcast_clamp_fusion), kind=kCustom, calls=%fused_computation | custom fusion | bytes 3153920 | tf_op jit(solution)/shard_map/jit(_take)/gather | solution.py:37
  229.2 5.3 convolution_negate_fusion
  234.5 0.0 reduce-scatter.5.cloned.1.call-start
  234.5 5.4 all-gather.5.cloned.1.call-done
  239.9 173.4 %reduce-scatter.3.cloned.1.call-done = f32[64,512]{1,0:T(8,128)} async-done(((f32[2048,512]{1,0:T(8,128)}), f32[64,512]{1,0:T(8,128)}) %reduce-scatter.3.cloned.1.call-update) | async-done | bytes 131088 | tf_op jit(solution)/shard_map/reduce_scatter | solution.py:44
  413.3 10.0 %negate_bitcast_fusion = f32[4096,512]{0,1:T(8,128)} fusion(f32[64,512]{1,0:T(8,128)} %reduce-scatter.3.cloned.1.call-done, f32[64,4096]{1,0:T(8,128)} %all-gather.5.cloned.1.call-done), kind=kOutput, calls=%fused_computation.2 | convolution fusion | flops 1612709888 | bytes 9568256 | tf_op jit(solution)/shard_map/dot_general | solution.py:15
  423.4 0.9 copy-done
  424.3 0.1 copy.16
  424.4 176.0 %reduce-scatter.5.cloned.1.call-done = f32[128,512]{0,1:T(8,128)} async-done(((f32[4096,512]{0,1:T(8,128)}), f32[128,512]{0,1:T(8,128)}) %reduce-scatter.5.cloned.1.call-update) | async-done | bytes 262160 | tf_op jit(solution)/shard_map/reduce_scatter | solution.py:48
  600.4 1.0 add.152
  601.4 0.8 copy.17
  (17 shorter events, 0.2 us)
Async XLA Ops:
  7.2 203.1 %all-gather.3.cloned.1.call-start = ((), (), s32[]{:S(2)}) async-start(), calls=%async_computation.3 | async-start | bytes 4325376 | tf_op jit(solution)/shard_map/all_gather | solution.py:39
  11.5 9.1 %copy-start.1 = (s32[16]{0:T(128)S(1)}, s32[16]{0:T(128)}, u32[]{:S(2)}) copy-start(s32[16]{0:T(128)} %param.5) | copy-start | bytes 196
  11.6 201.9 %all-to-all-start = ((f32[8,192,768]{2,1,0:T(8,128)}), f32[8,192,768]{2,1,0:T(8,128)}, u32[]{:S(2)}, u32[]{:S(2)}) async-start(f32[8,192,768]{2,1,0:T(8,128)} %stack.2), calls=%async_computation | async-start | bytes 9437184 | tf_op jit(solution)/shard_map/all_to_all | solution.py:11
  19.8 220.1 %all-gather.5.cloned.1.call-start = ((), (), s32[]{:S(2)}) async-start(), calls=%async_computation.5 | async-start | bytes 1179648 | tf_op jit(solution)/shard_map/all_gather | solution.py:47
  20.5 392.8 %reduce-scatter.3.cloned.1.call-start = ((), (), s32[]{:S(2)}) async-start(), calls=%async_computation.4 | async-start | bytes 4325376 | tf_op jit(solution)/shard_map/reduce_scatter | solution.py:44
  234.5 365.9 %reduce-scatter.5.cloned.1.call-start = ((), (), s32[]{:S(2)}) async-start(), calls=%async_computation.6 | async-start | bytes 8650752 | tf_op jit(solution)/shard_map/reduce_scatter | solution.py:48
  423.3 0.9 copy-start
Sparse Core Ops, SparseCore 0:
  9.8 200.3 all-gather.2
  212.1 27.8 all-gather.4
  243.1 170.2 reduce-scatter.2
  423.5 176.8 reduce-scatter.4
